TPU v7x, 128 devices: a whole 4x4x4 slice. The times are simulated.
128 devices in a mesh: mb: 4 (over y), feat: 32 (over z, x, core).
Axes of the slice: x: 4, y: 4, z: 4, core: 2. Of those that a mesh axis runs over, the one named last changes fastest.
Arguments:
- features: float32 [1024, 262144], P('feat', 'mb'), may hold values from -6 to 6
- tile_rows: int32 [768], P('mb'), may hold values from 0 to 127
- tile_cols: int32 [768], P('mb'), may hold values from 0 to 511
- tile_masks: int32 [768, 128, 128], P('mb'), may hold values 0 or 1
- weight: bfloat16 [1024, 256], replicated, may hold values from -0.5625 to 0.5625
- upstream: bfloat16 [65536, 256], P(('mb', 'feat')), may hold values from -6 to 6
Outputs:
- activation: bfloat16 [65536, 256], P(('mb', 'feat'))
- weight_grad: float32 [1024, 256], P('feat')
All inputs are finite; a program needn't handle non-finite values. No bound on the sum of `tile_masks` on one device may be relied on, other than what follows from the above.
Results may differ from a plain program's by a relative error of at most 0.0063.
Values may be sent and summed in bfloat16 or wider, within the bound.
No kernel may reach another device: no remote copies, remote signals or barrier semaphores. Data moves between devices by JAX's collectives and lax.ppermute only.
A program may use at most 128 MiB of HBM per device.

v0:
```python
import jax
import jax.numpy as jnp
from jax import lax
from jax.sharding import PartitionSpec as P

NT = 16384


def smooth_gate(values):
    return 0.5 * values * (1.0 + lax.erf(values * 0.7071067811865476))


def gate_slope(values):
    return (
        0.5 * (1.0 + lax.erf(values * 0.7071067811865476))
        + values * jnp.exp(-0.5 * values * values) * 0.3989422804014327
    )


def neighbor_mean(sources, row_index, col_index, masks):
    feat_cols = sources.shape[0]
    src_count = sources.shape[1]
    tile_size = masks.shape[1]
    row_tiles = NT // tile_size
    blocks = sources.reshape(feat_cols, src_count // tile_size, tile_size)
    picked = jnp.take(blocks, col_index, axis=1)
    weights = masks.astype(jnp.float32)
    contrib = jnp.einsum("fts,tds->tfd", picked, weights, precision=lax.Precision.HIGHEST)
    onehot = (row_index[None, :] == jnp.arange(row_tiles, dtype=jnp.int32)[:, None]).astype(
        jnp.float32
    )
    summed = jnp.einsum("rt,tfd->frd", onehot, contrib, precision=lax.Precision.HIGHEST).reshape(
        feat_cols, NT
    )
    degree = jnp.dot(onehot, jnp.sum(weights, axis=2), precision=lax.Precision.HIGHEST).reshape(NT)
    return ((sources[:, :NT] + summed) / (degree[None, :] + 1.0)).astype(jnp.bfloat16)


def per_device(features, tile_rows, tile_cols, tile_masks, weight, upstream):
    hidden_t = neighbor_mean(features, tile_rows, tile_cols, tile_masks)
    feat_cols = hidden_t.shape[0]
    weight_part = lax.dynamic_slice_in_dim(weight, lax.axis_index("feat") * feat_cols, feat_cols, 0)
    picked = hidden_t
    preact = lax.psum_scatter(
        lax.dot_general(
            picked, weight_part, (((0,), (0,)), ((), ())), preferred_element_type=jnp.float32
        ),
        "feat",
        scatter_dimension=0,
        tiled=True,
    )
    slopes = (upstream.astype(jnp.float32) * gate_slope(preact)).astype(jnp.bfloat16)
    picked = hidden_t
    local_grad = jnp.dot(
        picked,
        lax.all_gather(slopes, "feat", axis=0, tiled=True),
        preferred_element_type=jnp.float32,
    )
    activation = smooth_gate(preact).astype(jnp.bfloat16)
    weight_grad = lax.psum(local_grad, "mb")
    return (activation, weight_grad)


def solution(mesh):
    return jax.shard_map(
        per_device,
        mesh=mesh,
        in_specs=(
            P("feat", "mb"),
            P("mb"),
            P("mb"),
            P("mb", None, None),
            P(),
            P(("mb", "feat"), None),
        ),
        out_specs=(P(("mb", "feat"), None), P("feat", None)),
        check_vma=False,
    )
```

profile of v0, /device:TPU:0, one launch (start us, length us, event | category | flops | bytes accessed | tf_op | source)
XLA Modules:
  0.0 273.4 jit_solution(18257796936870843259)
XLA Ops:
  7.2 0.0 copy-start
  7.2 0.0 reduce-scatter.2.cloned.1.call-start
  7.2 0.7 compare_and_fusion
  8.0 0.7 compare_select_fusion
  8.7 7.9 %convert_reduce_fusion = f32[192,128]{1,0:T(8,128)S(1)} fusion(s32[192,128,128]{2,1,0:T(8,128)} %param.9), kind=kLoop, calls=%fused_computation.1 | loop fusion | flops 6266880 | bytes 12681216 | tf_op jit(solution)/shard_map/reduce_sum | solution.py:35
  16.5 0.0 copy-start.3
  16.6 7.8 %copy_bitcast_fusion = f32[32,512,128]{2,0,1:T(8,128)} fusion(f32[32,65536]{1,0:T(8,128)} %param.6), kind=kLoop, calls=%fused_computation.4 | loop fusion | bytes 16777216 | tf_op jit(solution)/shard_map/reshape | solution.py:25
  24.4 0.0 copy-done.3
  24.4 0.4 fusion.13
  24.8 5.9 %gather_fusion = f32[192,32,128]{2,1,0:T(8,128)} fusion(f32[32,512,128]{2,0,1:T(8,128)} %copy_bitcast_fusion, s32[1024]{0:T(1024)S(1)} %pad_clamp_fusion), kind=kCustom, calls=%fused_computation | custom fusion | bytes 6292224 | tf_op jit(solution)/shard_map/jit(_take)/gather | solution.py:26
  30.6 22.4 %fusion = f32[192,32,128]{2,1,0:T(8,128)S(1)} fusion(s32[192,128,128]{2,1,0:T(8,128)} %param.9, f32[192,32,128]{2,1,0:T(8,128)} %gather_fusion, pred[192]{0:T(512)(128)(4,1)S(1)} %compare_and_fusion), kind=kOutput, calls=%fused_computation.2 | convolution fusion | flops 1211891712 | bytes 18874560 | tf_op jit(solution)/shard_map/fts,tds->tfd/dot_general | solution.py:28
  53.1 4.7 %fusion.8 = f32[32,128,128]{1,2,0:T(8,128)S(1)} fusion(f32[192,32,128]{2,1,0:T(8,128)S(1)} %fusion, s32[192]{0:T(256)S(1)} %copy-done.3), kind=kOutput, calls=%fused_computation.12 | convolution fusion | flops 1207984128 | bytes 5243648 | tf_op jit(solution)/shard_map/rt,tfd->frd/dot_general | solution.py:32
  57.8 1.9 copy.11
  59.6 3.5 %fusion.7 = bf16[32,16384]{1,0:T(8,128)(2,1)S(1)} fusion(f32[4,8,128,128]{3,2,1,0:T(8,128)} %bitcast.26, f32[32,65536]{1,0:T(8,128)} %param.6, f32[16384]{0:T(1024)S(1)} %fusion.13), kind=kLoop, calls=%fused_computation.11 | loop fusion | flops 1572864 | bytes 5308416 | tf_op jit(solution)/shard_map/convert_element_type | solution.py:36
  63.1 0.0 copy-done
  63.1 8.1 %fusion.24 = f32[16384,256]{1,0:T(8,128)} fusion(bf16[32,16384]{1,0:T(8,128)(2,1)S(1)} %fusion.7, bf16[1024,256]{1,0:T(8,128)(2,1)S(1)} %copy-done, s32[]{:T(128)S(6)} %select_n.14), kind=kOutput, calls=%fused_computation.30 | convolution fusion | flops 268435456 | bytes 17842180 | tf_op jit(solution)/shard_map/dot_general | solution.py:45
  71.2 0.0 copy-start.2
  71.2 0.0 reduce-scatter.2.cloned.1.call-update
  71.3 0.0 all-gather.2.cloned.1.call-start
  71.3 118.2 %reduce-scatter.2.cloned.1.call-done = f32[512,256]{1,0:T(8,128)} async-done(((f32[16384,256]{1,0:T(8,128)}), f32[512,256]{1,0:T(8,128)}) %reduce-scatter.2.cloned.1.call-update) | async-done | bytes 524304 | tf_op jit(solution)/shard_map/reduce_scatter | solution.py:44
  189.5 0.0 copy-done.2
  189.5 2.1 fusion.19
  191.7 0.0 all-gather.2.cloned.1.call-update
  191.7 52.2 %all-gather.2.cloned.1.call-done = bf16[16384,256]{1,0:T(8,128)(2,1)} async-done(((bf16[512,256]{1,0:T(8,128)(2,1)}), bf16[16384,256]{1,0:T(8,128)(2,1)}) %all-gather.2.cloned.1.call-update) | async-done | bytes 8388624 | tf_op jit(solution)/shard_map/all_gather | solution.py:56
  243.9 0.0 copy-start.1
  243.9 5.0 %fusion.28 = f32[32,256]{1,0:T(8,128)S(1)} fusion(bf16[32,16384]{1,0:T(8,128)(2,1)S(1)} %fusion.7, bf16[16384,256]{1,0:T(8,128)(2,1)} %all-gather.2.cloned.1.call-done), kind=kOutput, calls=%fused_computation.37 | convolution fusion | flops 268435456 | bytes 9469952 | tf_op jit(solution)/shard_map/dot_general | solution.py:54
  248.9 17.6 %psum.7 = f32[32,256]{1,0:T(8,128)} all-reduce(f32[32,256]{1,0:T(8,128)S(1)} %fusion.28), channel_id=1, replica_groups=mesh['mb'=4,'feat'=32] {'mb'}, use_global_device_ids=true, to_apply=%region_2.3 | all-reduce | flops 8192 | bytes 65536 | tf_op jit(solution)/shard_map/psum | solution.py:60
  266.5 0.0 copy-done.1
  (1 shorter events, 0.0 us)
Async XLA Ops:
  7.2 55.9 %copy-start = (bf16[1024,256]{1,0:T(8,128)(2,1)S(1)}, bf16[1024,256]{1,0:T(8,128)(2,1)}, u32[]{:S(2)}) copy-start(bf16[1024,256]{1,0:T(8,128)(2,1)} %param.10) | copy-start | bytes 1572868
  7.2 182.4 %reduce-scatter.2.cloned.1.call-start = ((), (), s32[]{:S(2)}) async-start(), calls=%async_computation.1 | async-start | bytes 17301504 | tf_op jit(solution)/shard_map/reduce_scatter | solution.py:44
  16.5 7.8 %copy-start.3 = (s32[192]{0:T(256)S(1)}, s32[192]{0:T(256)}, u32[]{:S(2)}) copy-start(s32[192]{0:T(256)} %param.7) | copy-start | bytes 2308
  71.2 118.3 %copy-start.2 = (bf16[512,256]{1,0:T(8,128)(2,1)S(1)}, bf16[512,256]{1,0:T(8,128)(2,1)}, u32[]{:S(2)}) copy-start(bf16[512,256]{1,0:T(8,128)(2,1)} %param.11) | copy-start | bytes 786436
  71.3 172.7 %all-gather.2.cloned.1.call-start = ((), (), s32[]{:S(2)}) async-start(), calls=%async_computation.2 | async-start | bytes 8650752 | tf_op jit(solution)/shard_map/all_gather | solution.py:56
  243.9 22.6 %copy-start.1 = (bf16[1024,256]{1,0:T(8,128)(2,1)S(1)}, bf16[1024,256]{1,0:T(8,128)(2,1)}, u32[]{:S(2)}) copy-start(bf16[1024,256]{1,0:T(8,128)(2,1)} %param.10) | copy-start | bytes 1572868
Sparse Core Ops, SparseCore 0:
  71.4 118.1 reduce-scatter.1
  191.8 52.0 all-gather.1
where the time goes:
time: 274 us; the launch traced here: 273 us
  waiting for transfers between devices  170 us (62%)
  matrix products  40.6 us (15%)
  blocking collectives  17.6 us (6%)
  local copies, waits for them, and re-layouts  15.6 us (6%)
  other arithmetic  14.9 us (5%)
  between operations  14.1 us (5%)
    reduce_scatter x1, waiting for transfers between devices, per_device(): lax.psum_scatter(lax.dot_general(picked, weight_part, (((0,), (0,)), ((),...  118 us
    all_gather x1, waiting for transfers between devices, per_device(): lax.all_gather(slopes, 'feat', axis=0, tiled=True)  52.2 us
    dot_general x1, matrix products, neighbor_mean(): jnp.einsum('fts,tds->tfd', picked, weights, precision=lax.Precision.HIGHEST)  22.4 us
    psum x1, blocking collectives, per_device(): weight_grad = lax.psum(local_grad, 'mb')  17.6 us
    dot_general x1, matrix products, per_device(): lax.dot_general(picked, weight_part, (((0,), (0,)), ((), ())), preferred_...  8.13 us
    reduce_sum x1, other arithmetic, neighbor_mean(): jnp.sum(weights, axis=2)  7.89 us
    reshape x1, local copies, waits for them, and re-layouts, neighbor_mean(): blocks = sources.reshape(feat_cols, src_count // tile_size, tile_size)  7.81 us
    gather x1, local copies, waits for them, and re-layouts, neighbor_mean(): picked = jnp.take(blocks, col_index, axis=1)  5.89 us
  transfers between devices with their start and end apart: 2, of which 2 were waited for; matrix products, arithmetic and copies ran while one was open for 0% of the time, Pallas kernels for 0%

commit v1 on v0

--- a/solution.py
+++ b/solution.py
@@ -51,11 +51,13 @@
     )
     slopes = (upstream.astype(jnp.float32) * gate_slope(preact)).astype(jnp.bfloat16)
     picked = hidden_t
-    local_grad = jnp.dot(
-        picked,
-        lax.all_gather(slopes, "feat", axis=0, tiled=True),
-        preferred_element_type=jnp.float32,
-    )
+
+    def mark_frame_over_axis(shard_in):
+        low = jnp.concatenate(tuple((shard_in for _ in range(lax.axis_size("feat")))), axis=0)
+        latest = lax.all_to_all(low, "feat", 0, 0, tiled=True)
+        return latest
+
+    local_grad = jnp.dot(picked, mark_frame_over_axis(slopes), preferred_element_type=jnp.float32)
     activation = smooth_gate(preact).astype(jnp.bfloat16)
     weight_grad = lax.psum(local_grad, "mb")
     return (activation, weight_grad)

time: 274 us -> 336 us (1.23)
  waiting for transfers between devices: 170 us -> 223 us
  starting transfers between devices: 0.08 us -> 5.53 us
  local copies, waits for them, and re-layouts: 15.6 us -> 19.4 us
    all_to_all x0 -> x1, waiting for transfers between devices: none -> 105 us  [mark_frame_over_axis(): latest = lax.all_to_all(low, 'feat', 0, 0, tiled=True)]
    all_gather x1 -> x0, waiting for transfers between devices: 52.2 us -> none  [per_device(): lax.all_gather(slopes, 'feat', axis=0, tiled=True)]
    all_to_all x0 -> x1, starting transfers between devices: none -> 5.49 us  [mark_frame_over_axis(): latest = lax.all_to_all(low, 'feat', 0, 0, tiled=True)]
    unnamed x8 -> x42, local copies, waits for them, and re-layouts: 0.03 us -> 3.83 us
where the time goes in v1:
time: 336 us
  waiting for transfers between devices  223 us (66%)
  matrix products  40.6 us (12%)
  local copies, waits for them, and re-layouts  19.4 us (6%)
  blocking collectives  17.6 us (5%)
  other arithmetic  14.8 us (4%)
  between operations  14.4 us (4%)
  starting transfers between devices  5.53 us (2%)
    reduce_scatter x1, waiting for transfers between devices, per_device(): lax.psum_scatter(lax.dot_general(picked, weight_part, (((0,), (0,)), ((),...  118 us
    all_to_all x1, waiting for transfers between devices, mark_frame_over_axis(): latest = lax.all_to_all(low, 'feat', 0, 0, tiled=True)  105 us
    dot_general x1, matrix products, neighbor_mean(): jnp.einsum('fts,tds->tfd', picked, weights, precision=lax.Precision.HIGHEST)  22.4 us
    psum x1, blocking collectives, per_device(): weight_grad = lax.psum(local_grad, 'mb')  17.6 us
    dot_general x1, matrix products, per_device(): lax.dot_general(picked, weight_part, (((0,), (0,)), ((), ())), preferred_...  8.12 us
    reduce_sum x1, other arithmetic, neighbor_mean(): jnp.sum(weights, axis=2)  7.89 us
    reshape x1, local copies, waits for them, and re-layouts, neighbor_mean(): blocks = sources.reshape(feat_cols, src_count // tile_size, tile_size)  7.81 us
  transfers between devices with their start and end apart: 2, of which 2 were waited for; matrix products, arithmetic and copies ran while one was open for 0% of the time, Pallas kernels for 0%

profile of v1, /device:TPU:0, one launch (start us, length us, event | category | flops | bytes accessed | tf_op | source)
XLA Modules:
  0.0 335.7 jit_solution(15606494299120997235)
XLA Ops:
  7.2 0.0 copy-start
  7.2 0.0 reduce-scatter.2.cloned.1.call-start
  7.2 0.7 compare_and_fusion
  8.0 0.7 compare_select_fusion
  8.7 7.9 %convert_reduce_fusion = f32[192,128]{1,0:T(8,128)S(1)} fusion(s32[192,128,128]{2,1,0:T(8,128)} %param.9), kind=kLoop, calls=%fused_computation.1 | loop fusion | flops 6266880 | bytes 12681216 | tf_op jit(solution)/shard_map/reduce_sum | solution.py:35
  16.5 0.0 copy-start.5
  16.6 7.8 %copy_bitcast_fusion = f32[32,512,128]{2,0,1:T(8,128)} fusion(f32[32,65536]{1,0:T(8,128)} %param.6), kind=kLoop, calls=%fused_computation.4 | loop fusion | bytes 16777216 | tf_op jit(solution)/shard_map/reshape | solution.py:25
  24.4 0.0 copy-done.5
  24.4 0.4 fusion.13
  24.7 5.9 %gather_fusion = f32[192,32,128]{2,1,0:T(8,128)} fusion(f32[32,512,128]{2,0,1:T(8,128)} %copy_bitcast_fusion, s32[1024]{0:T(1024)S(1)} %pad_clamp_fusion), kind=kCustom, calls=%fused_computation | custom fusion | bytes 6292224 | tf_op jit(solution)/shard_map/jit(_take)/gather | solution.py:26
  30.6 22.4 %fusion = f32[192,32,128]{2,1,0:T(8,128)S(1)} fusion(s32[192,128,128]{2,1,0:T(8,128)} %param.9, f32[192,32,128]{2,1,0:T(8,128)} %gather_fusion, pred[192]{0:T(512)(128)(4,1)S(1)} %compare_and_fusion), kind=kOutput, calls=%fused_computation.2 | convolution fusion | flops 1211891712 | bytes 18874560 | tf_op jit(solution)/shard_map/fts,tds->tfd/dot_general | solution.py:28
  53.1 4.7 %fusion.8 = f32[32,128,128]{1,2,0:T(8,128)S(1)} fusion(f32[192,32,128]{2,1,0:T(8,128)S(1)} %fusion, s32[192]{0:T(256)S(1)} %copy-done.5), kind=kOutput, calls=%fused_computation.12 | convolution fusion | flops 1207984128 | bytes 5243648 | tf_op jit(solution)/shard_map/rt,tfd->frd/dot_general | solution.py:32
  57.8 1.9 copy.11
  59.6 3.5 %fusion.7 = bf16[32,16384]{1,0:T(8,128)(2,1)S(1)} fusion(f32[4,8,128,128]{3,2,1,0:T(8,128)} %bitcast.29, f32[32,65536]{1,0:T(8,128)} %param.6, f32[16384]{0:T(1024)S(1)} %fusion.13), kind=kLoop, calls=%fused_computation.11 | loop fusion | flops 1572864 | bytes 5308416 | tf_op jit(solution)/shard_map/convert_element_type | solution.py:36
  63.1 0.0 copy-done
  63.1 8.1 %fusion.24 = f32[16384,256]{1,0:T(8,128)} fusion(bf16[32,16384]{1,0:T(8,128)(2,1)S(1)} %fusion.7, bf16[1024,256]{1,0:T(8,128)(2,1)S(1)} %copy-done, s32[]{:T(128)S(6)} %select_n.14), kind=kOutput, calls=%fused_computation.62 | convolution fusion | flops 268435456 | bytes 17842180 | tf_op jit(solution)/shard_map/dot_general | solution.py:45
  71.2 0.0 copy-start.4
  71.2 0.0 reduce-scatter.2.cloned.1.call-update
  71.2 118.3 %reduce-scatter.2.cloned.1.call-done = f32[512,256]{1,0:T(8,128)} async-done(((f32[16384,256]{1,0:T(8,128)}), f32[512,256]{1,0:T(8,128)}) %reduce-scatter.2.cloned.1.call-update) | async-done | bytes 524304 | tf_op jit(solution)/shard_map/reduce_scatter | solution.py:44
  189.5 0.0 copy-done.4
  189.5 1.3 constant_dynamic-update-slice_fusion.31
  191.6 0.0 copy-start.2
  191.7 3.2 copy-done.2
  194.9 0.0 copy-start.3
  194.9 5.5 %all-to-all-start = ((bf16[32,512,256]{2,1,0:T(8,128)(2,1)}), bf16[32,512,256]{2,1,0:T(8,128)(2,1)}, u32[]{:S(2)}, u32[]{:S(2)}) async-start(bf16[32,512,256]{2,1,0:T(8,128)(2,1)} %bitcast.28), calls=%async_computation.1 | async-start | bytes 16777216 | tf_op jit(solution)/shard_map/all_to_all | solution.py:57
  200.4 0.0 copy-done.3
  200.4 0.8 multiply_convert_fusion
  201.2 105.0 %all-to-all-done = bf16[32,512,256]{2,1,0:T(8,128)(2,1)} async-done(((bf16[32,512,256]{2,1,0:T(8,128)(2,1)}), bf16[32,512,256]{2,1,0:T(8,128)(2,1)}, u32[]{:S(2)}, u32[]{:S(2)}) %all-to-all-start) | async-done | bytes 8388640 | tf_op jit(solution)/shard_map/all_to_all | solution.py:57
  306.2 0.0 copy-start.1
  306.2 5.0 %fusion.29 = f32[32,256]{1,0:T(8,128)S(1)} fusion(bf16[32,16384]{1,0:T(8,128)(2,1)S(1)} %fusion.7, bf16[16384,256]{1,0:T(8,128)(2,1)} %bitcast.5), kind=kOutput, calls=%fused_computation.69 | convolution fusion | flops 268435456 | bytes 9469952 | tf_op jit(solution)/shard_map/dot_general | solution.py:60
  311.2 17.6 %psum.7 = f32[32,256]{1,0:T(8,128)} all-reduce(f32[32,256]{1,0:T(8,128)S(1)} %fusion.29), channel_id=1, replica_groups=mesh['mb'=4,'feat'=32] {'mb'}, use_global_device_ids=true, to_apply=%region_2.3 | all-reduce | flops 8192 | bytes 65536 | tf_op jit(solution)/shard_map/psum | solution.py:62
  328.8 0.0 copy-done.1
  (32 shorter events, 0.6 us)
Async XLA Ops:
  7.2 55.9 %copy-start = (bf16[1024,256]{1,0:T(8,128)(2,1)S(1)}, bf16[1024,256]{1,0:T(8,128)(2,1)}, u32[]{:S(2)}) copy-start(bf16[1024,256]{1,0:T(8,128)(2,1)} %param.10) | copy-start | bytes 1572868
  7.2 182.3 %reduce-scatter.2.cloned.1.call-start = ((), (), s32[]{:S(2)}) async-start(), calls=%async_computation.2 | async-start | bytes 17301504 | tf_op jit(solution)/shard_map/reduce_scatter | solution.py:44
  16.5 7.8 %copy-start.5 = (s32[192]{0:T(256)S(1)}, s32[192]{0:T(256)}, u32[]{:S(2)}) copy-start(s32[192]{0:T(256)} %param.7) | copy-start | bytes 2308
  71.2 118.3 %copy-start.4 = (bf16[512,256]{1,0:T(8,128)(2,1)S(1)}, bf16[512,256]{1,0:T(8,128)(2,1)}, u32[]{:S(2)}) copy-start(bf16[512,256]{1,0:T(8,128)(2,1)} %param.11) | copy-start | bytes 786436
  191.6 3.2 copy-start.2
  194.9 5.5 %copy-start.3 = (f32[512,256]{1,0:T(8,128)S(1)}, f32[512,256]{1,0:T(8,128)}, u32[]{:S(2)}) copy-start(f32[512,256]{1,0:T(8,128)} %reduce-scatter.2.cloned.1.call-done) | copy-start | bytes 1572868
  194.9 111.4 %all-to-all-start = ((bf16[32,512,256]{2,1,0:T(8,128)(2,1)}), bf16[32,512,256]{2,1,0:T(8,128)(2,1)}, u32[]{:S(2)}, u32[]{:S(2)}) async-start(bf16[32,512,256]{2,1,0:T(8,128)(2,1)} %bitcast.28), calls=%async_computation.1 | async-start | bytes 16777216 | tf_op jit(solution)/shard_map/all_to_all | solution.py:57
  306.2 22.6 %copy-start.1 = (bf16[1024,256]{1,0:T(8,128)(2,1)S(1)}, bf16[1024,256]{1,0:T(8,128)(2,1)}, u32[]{:S(2)}) copy-start(bf16[1024,256]{1,0:T(8,128)(2,1)} %param.10) | copy-start | bytes 1572868
Sparse Core Ops, SparseCore 0:
  71.4 118.1 reduce-scatter.1
